TPU v7x, 512 devices: a whole 4x4x16 slice. The times are simulated.
512 devices in a mesh: tm: 32 (over y, z_lo), lon: 16 (over x, z_hi, core).
Axes of the slice: x: 4, y: 4, z: 16 (z_hi: 2, z_lo: 8; z = z_hi * 8 + z_lo), core: 2. Of those that a mesh axis runs over, the one named last changes fastest.
Arguments:
- field: bfloat16 [4096, 288, 512], P('tm', 'lon'), may hold values from -15 to 15
- omega: bfloat16 [288, 512, 64], P('lon'), may hold values from -0.015625 to 0.015625
Outputs:
- projected: bfloat16 [4096, 288, 512], P('tm', 'lon')
- series: float32 [4096, 64], P('tm')
All inputs are finite; a program needn't handle non-finite values.
Results may differ from a plain program's by a relative error of at most 0.0082.
Values may be sent and summed in bfloat16 or wider, within the bound.
A program may use at most 64 MiB of HBM per device.

v0:
```python
import math
import jax
import jax.numpy as jnp
from jax import lax
from jax.sharding import PartitionSpec as P

NLAT = 32
NVAR = 16
HALF = 15
RANK = 64


def with_halo(block, sides, width, periodic):
    for axis, dim in sides:
        count = lax.axis_size(axis)
        forward = [(i, i + 1) for i in range(count - 1)]
        if periodic:
            forward.append((count - 1, 0))
        backward = [(target, source) for source, target in forward]
        low = lax.ppermute(
            lax.slice_in_dim(block, block.shape[dim] - width, None, axis=dim), axis, forward
        )
        high = lax.ppermute(lax.slice_in_dim(block, 0, width, axis=dim), axis, backward)
        block = jnp.concatenate([low, block, high], axis=dim)
    return block


def band_taps(half):
    offsets = jnp.arange(-half, half + 1).astype(jnp.float32)
    safe = jnp.where(offsets == 0, 1.0, offsets)
    core = (jnp.sin(2.0 * math.pi * safe / 3.0) - jnp.sin(2.0 * math.pi * safe / 30.0)) / (
        math.pi * safe
    )
    core = jnp.where(offsets == 0, 2.0 * (1.0 / 3.0 - 1.0 / 30.0), core)
    spread = math.pi * safe / (half + 1)
    sigma = jnp.where(offsets == 0, 1.0, jnp.sin(spread) / spread)
    return (core * sigma).astype(jnp.bfloat16)


def local(field, omega):
    days, lon_dev, cols = field.shape
    width = lon_dev * cols
    extended = with_halo(field, (("tm", 0),), HALF, False)
    extended = with_halo(extended, (("lon", 1),), 1, True)
    taps = band_taps(HALF).astype(jnp.float32)
    row_index = lax.broadcasted_iota(jnp.int32, (days, days + 2 * HALF), 0)
    col_index = lax.broadcasted_iota(jnp.int32, (days, days + 2 * HALF), 1)
    offset = col_index - row_index
    tap_index = jnp.arange(2 * HALF + 1, dtype=jnp.int32)
    toeplitz = jnp.sum(jnp.where(offset[:, :, None] == tap_index, taps, 0.0), axis=-1).astype(
        jnp.bfloat16
    )
    filtered = jnp.einsum("ij,jlc->ilc", toeplitz, extended, preferred_element_type=jnp.float32)
    across = filtered[:, :-2] + 2.0 * filtered[:, 1:-1] + filtered[:, 2:]
    grid = across.reshape(days, lon_dev, NVAR, NLAT)
    lat_pad = jnp.pad(grid, ((0, 0), (0, 0), (0, 0), (1, 1)))
    smooth = (lat_pad[..., :-2] + 2.0 * lat_pad[..., 1:-1] + lat_pad[..., 2:]) * 0.0625
    anomalies = smooth.reshape(days, width).astype(jnp.bfloat16)
    flat_omega = omega.reshape(width, RANK)
    partial_sketch = jnp.dot(anomalies, flat_omega, preferred_element_type=jnp.float32)
    sketch = lax.psum(partial_sketch, "lon")
    local_gram = jnp.dot(sketch.T, sketch, precision=lax.Precision.HIGHEST)
    gram = lax.psum(local_gram, "tm")
    lower = jnp.linalg.cholesky(gram)
    basis = jax.scipy.linalg.solve_triangular(lower, sketch.T, lower=True).T
    series = basis * math.sqrt(days * lax.axis_size("tm"))
    basis_b = basis.astype(jnp.bfloat16)
    terms = jnp.einsum("ts,tk->sk", anomalies, basis_b, preferred_element_type=jnp.float32)
    patterns = lax.psum(terms, "tm").astype(jnp.bfloat16)
    projected = jnp.einsum(
        "tk,sk->ts", basis_b, patterns, preferred_element_type=jnp.float32
    ).astype(jnp.bfloat16)
    return (projected.reshape(days, lon_dev, cols), series)


def solution(mesh):
    in_specs = (P("tm", "lon", None), P("lon", None, None))
    out_specs = (P("tm", "lon", None), P("tm", None))
    return jax.shard_map(local, mesh=mesh, in_specs=in_specs, out_specs=out_specs, check_vma=False)
```

profile of v0, /device:TPU:4, one launch (start us, length us, event | category | flops | bytes accessed | tf_op | source)
XLA Modules:
  0.0 712.1 jit_solution(13577348520286733900)
XLA Ops:
  0.6 1.3 fusion.27
  1.9 3.8 collective-permute-start
  5.8 1.3 collective-permute-start.1
  7.1 1.4 copy.20
  8.5 0.1 convert_convert_fusion
  8.6 3.5 collective-permute-done
  12.0 10.3 %collective-permute-done.1 = bf16[15,18,512]{2,0,1:T(8,128)(2,1)S(1)} collective-permute-done((bf16[15,18,512]{2,0,1:T(8,128)(2,1)S(1)}, bf16[15,18,512]{2,0,1:T(8,128)(2,1)S(1)}, u32[]{:S(2)}, u32[]{:S(2)}) %collective-permute-start.1) | collective-permute-done | bytes 276512 | tf_op jit(solution)/shard_map/ppermute | solution.py:23
  22.3 0.1 pad_maximum_fusion.2
  22.4 1.9 collective-permute-start.2
  24.3 13.3 %collective-permute-start.3 = (bf16[158,1,512]{2,0,1:T(8,128)(2,1)S(1)}, bf16[158,1,512]{2,0,1:T(8,128)(2,1)S(1)}, u32[]{:S(2)}, u32[]{:S(2)}) collective-permute-start(bf16[158,1,512]{2,0,1:T(8,128)(2,1)S(1)} %get-tuple-element.9), channel_id=1, source_target_pairs={{1,0},{2,1},{3,2},{4,3},{5,4},{6,5},{7,6},{8,7},{9,8},{10,9},{11,1... | collective-permute-start | bytes 485384 | tf_op jit(solution)/shard_map/ppermute | solution.py:23
  37.6 0.3 select_reduce_fusion
  37.9 0.9 collective-permute-done.2
  38.8 6.9 collective-permute-done.3
  45.7 1.0 fusion.5
  46.6 2.8 slice_add_fusion
  49.5 6.1 copy.13
  55.6 6.7 fusion.3
  62.3 1.2 fusion.29
  63.5 125.3 %psum.21 = f32[128,64]{0,1:T(8,128)S(1)} all-reduce(f32[128,64]{0,1:T(8,128)} %fusion.29), channel_id=1, replica_groups=mesh['tm'=32,'lon'=16] {'lon'}, use_global_device_ids=true, to_apply=%region_1.2 | all-reduce | flops 8192 | bytes 65536 | tf_op jit(solution)/shard_map/psum | solution.py:61
  188.7 0.2 fusion.28
  188.9 231.2 %psum.22 = f32[64,64]{0,1:T(8,128)S(1)} all-reduce(f32[64,64]{0,1:T(8,128)S(1)} %fusion.28), channel_id=1, replica_groups=mesh['tm'=32,'lon'=16] {'tm'}, use_global_device_ids=true, to_apply=%region_2.3 | all-reduce | flops 4096 | bytes 32768 | tf_op jit(solution)/shard_map/psum | solution.py:63
  420.2 0.1 copy.16
  420.3 5.8 cholesky.16
  426.1 0.6 compare_reduce_fusion
  426.8 0.7 fusion.18
  427.4 4.9 custom-call.7
  432.3 0.9 broadcast_multiply_fusion
  433.2 2.3 fusion.23
  435.6 269.1 %all-reduce.2 = bf16[9216,64]{0,1:T(8,128)(2,1)S(1)} all-reduce(f32[9216,64]{0,1:T(8,128)} %fusion.23), channel_id=1, replica_groups=mesh['tm'=32,'lon'=16] {'tm'}, use_global_device_ids=true, to_apply=%region_5.6 | all-reduce | flops 589824 | bytes 3538944 | tf_op jit(solution)/shard_map/psum | solution.py:69
  704.6 0.8 convolution_convert_fusion
  705.4 2.4 copy.17
  707.9 4.3 copy.18
  (5 shorter events, 0.1 us)
Async XLA Ops:
  0.6 21.6 %copy-start = (bf16[128,18,512]{2,0,1:T(8,128)(2,1)S(1)}, bf16[128,18,512]{2,0,1:T(8,128)(2,1)}, u32[]{:S(2)}) copy-start(bf16[128,18,512]{2,0,1:T(8,128)(2,1)} %param.2) | copy-start | bytes 7077892
  1.9 10.1 %collective-permute-start = (bf16[15,18,512]{2,0,1:T(8,128)(2,1)S(1)}, bf16[15,18,512]{2,0,1:T(8,128)(2,1)S(1)}, u32[]{:S(2)}, u32[]{:S(2)}) collective-permute-start(bf16[15,18,512]{2,0,1:T(8,128)(2,1)S(1)} %get-tuple-element.10), channel_id=1, source_target_pairs={{0,16},{16,32},{32,48},{48,64},{64,80},{80,96},{96,112},{112,128},... | collective-permute-start | bytes 829448 | tf_op jit(solution)/shard_map/ppermute | solution.py:20
  5.8 16.5 %collective-permute-start.1 = (bf16[15,18,512]{2,0,1:T(8,128)(2,1)S(1)}, bf16[15,18,512]{2,0,1:T(8,128)(2,1)S(1)}, u32[]{:S(2)}, u32[]{:S(2)}) collective-permute-start(bf16[15,18,512]{2,0,1:T(8,128)(2,1)S(1)} %get-tuple-element.11), channel_id=1, source_target_pairs={{16,0},{32,16},{48,32},{64,48},{80,64},{96,80},{112,96},{128,112},... | collective-permute-start | bytes 829448 | tf_op jit(solution)/shard_map/ppermute | solution.py:23
  22.4 16.4 %collective-permute-start.2 = (bf16[158,1,512]{2,0,1:T(8,128)(2,1)S(1)}, bf16[158,1,512]{2,0,1:T(8,128)(2,1)S(1)}, u32[]{:S(2)}, u32[]{:S(2)}) collective-permute-start(bf16[158,1,512]{2,0,1:T(8,128)(2,1)S(1)} %get-tuple-element.8), channel_id=1, source_target_pairs={{0,1},{1,2},{2,3},{3,4},{4,5},{5,6},{6,7},{7,8},{8,9},{9,10},{10,1... | collective-permute-start | bytes 485384 | tf_op jit(solution)/shard_map/ppermute | solution.py:20
  24.3 21.4 %collective-permute-start.3 = (bf16[158,1,512]{2,0,1:T(8,128)(2,1)S(1)}, bf16[158,1,512]{2,0,1:T(8,128)(2,1)S(1)}, u32[]{:S(2)}, u32[]{:S(2)}) collective-permute-start(bf16[158,1,512]{2,0,1:T(8,128)(2,1)S(1)} %get-tuple-element.9), channel_id=1, source_target_pairs={{1,0},{2,1},{3,2},{4,3},{5,4},{6,5},{7,6},{8,7},{9,8},{10,9},{11,1... | collective-permute-start | bytes 485384 | tf_op jit(solution)/shard_map/ppermute | solution.py:23
where the time goes:
time: 713 us; the launch traced here: 712 us
  blocking collectives  626 us (88%)
  other arithmetic  22.1 us (3%)
  waiting for transfers between devices  21.5 us (3%)
  starting transfers between devices  20.3 us (3%)
  local copies, waits for them, and re-layouts  15.6 us (2%)
    psum x1, blocking collectives, local(): patterns = lax.psum(terms, 'tm').astype(jnp.bfloat16)  269 us
    psum x1, blocking collectives, local(): gram = lax.psum(local_gram, 'tm')  231 us
    psum x1, blocking collectives, local(): sketch = lax.psum(partial_sketch, 'lon')  125 us
    ppermute x2, waiting for transfers between devices, with_halo(): lax.ppermute(lax.slice_in_dim(block, 0, width, axis=dim), axis, backward)  17.2 us
    ppermute x2, starting transfers between devices, with_halo(): lax.ppermute(lax.slice_in_dim(block, 0, width, axis=dim), axis, backward)  14.5 us
  transfers between devices with their start and end apart: 4, of which 4 were waited for; matrix products, arithmetic and copies ran while one was open for 0% of the time, Pallas kernels for 0%

commit v1 on v0

--- a/solution.py
+++ b/solution.py
@@ -58,7 +58,7 @@
     anomalies = smooth.reshape(days, width).astype(jnp.bfloat16)
     flat_omega = omega.reshape(width, RANK)
     partial_sketch = jnp.dot(anomalies, flat_omega, preferred_element_type=jnp.float32)
-    sketch = lax.psum(partial_sketch, "lon")
+    sketch = jnp.sum(lax.all_gather(partial_sketch, "lon"), axis=0)
     local_gram = jnp.dot(sketch.T, sketch, precision=lax.Precision.HIGHEST)
     gram = lax.psum(local_gram, "tm")
     lower = jnp.linalg.cholesky(gram)

time: 713 us -> 636 us (0.89)
  the two profiles are of different devices: /device:TPU:4 before, /device:TPU:6 now
where the time goes in v1:
time: 636 us; the launch traced here: 635 us
  blocking collectives  550 us (86%)
  other arithmetic  22.2 us (3%)
  waiting for transfers between devices  20.8 us (3%)
  starting transfers between devices  20.3 us (3%)
  local copies, waits for them, and re-layouts  15.7 us (2%)
    psum x1, blocking collectives, local(): patterns = lax.psum(terms, 'tm').astype(jnp.bfloat16)  268 us
    psum x1, blocking collectives, local(): gram = lax.psum(local_gram, 'tm')  225 us
    all_gather x1, blocking collectives, local(): sketch = jnp.sum(lax.all_gather(partial_sketch, 'lon'), axis=0)  56.5 us
    ppermute x2, waiting for transfers between devices, with_halo(): lax.ppermute(lax.slice_in_dim(block, 0, width, axis=dim), axis, backward)  16.4 us
    ppermute x2, starting transfers between devices, with_halo(): lax.ppermute(lax.slice_in_dim(block, 0, width, axis=dim), axis, backward)  14.5 us
  transfers between devices with their start and end apart: 4, of which 4 were waited for; matrix products, arithmetic and copies ran while one was open for 0% of the time, Pallas kernels for 0%

profile of v1, /device:TPU:6, one launch (start us, length us, event | category | flops | bytes accessed | tf_op | source)
XLA Modules:
  0.0 635.1 jit_solution(10738277777765853522)
XLA Ops:
  0.6 1.3 fusion.27
  1.9 3.8 collective-permute-start
  5.8 1.3 collective-permute-start.1
  7.1 1.4 copy.26
  8.6 3.5 collective-permute-done
  12.0 10.3 %collective-permute-done.1 = bf16[15,18,512]{2,0,1:T(8,128)(2,1)S(1)} collective-permute-done((bf16[15,18,512]{2,0,1:T(8,128)(2,1)S(1)}, bf16[15,18,512]{2,0,1:T(8,128)(2,1)S(1)}, u32[]{:S(2)}, u32[]{:S(2)}) %collective-permute-start.1) | collective-permute-done | bytes 276512 | tf_op jit(solution)/shard_map/ppermute | solution.py:23
  22.3 0.1 pad_maximum_fusion.2
  22.4 1.9 collective-permute-start.2
  24.3 13.3 %collective-permute-start.3 = (bf16[158,1,512]{2,0,1:T(8,128)(2,1)S(1)}, bf16[158,1,512]{2,0,1:T(8,128)(2,1)S(1)}, u32[]{:S(2)}, u32[]{:S(2)}) collective-permute-start(bf16[158,1,512]{2,0,1:T(8,128)(2,1)S(1)} %get-tuple-element.11), channel_id=1, source_target_pairs={{1,0},{2,1},{3,2},{4,3},{5,4},{6,5},{7,6},{8,7},{9,8},{10,9},{11,1... | collective-permute-start | bytes 485384 | tf_op jit(solution)/shard_map/ppermute | solution.py:23
  37.6 0.3 select_reduce_fusion
  37.9 0.9 collective-permute-done.2
  38.8 6.2 collective-permute-done.3
  44.9 1.0 fusion.5
  45.9 2.8 slice_add_fusion
  48.7 6.1 copy.19
  54.8 6.7 %fusion.3 = bf16[128,18,16,32]{0,3,2,1:T(8,128)(2,1)S(1)} fusion(f32[128,18,16,32]{0,3,2,1:T(8,128)} %bitcast.35), kind=kLoop, calls=%fused_computation.6 | loop fusion | flops 5898240 | bytes 7077888 | tf_op jit(solution)/shard_map/convert_element_type | solution.py:58
  61.5 0.5 fusion.29
  62.1 56.5 %all-gather = f32[2048,64]{0,1:T(8,128)S(1)} all-gather(f32[128,64]{0,1:T(8,128)S(1)} %fusion.29), channel_id=2, replica_groups=mesh['tm'=32,'lon'=16] {'lon'}, dimensions={0}, use_global_device_ids=true | all-gather | bytes 557056 | tf_op jit(solution)/shard_map/all_gather | solution.py:61
  118.6 0.1 copy.27
  118.7 0.1 bitcast_reduce_fusion
  118.8 0.2 fusion.28
  119.0 225.1 %psum.14 = f32[64,64]{0,1:T(8,128)S(1)} all-reduce(f32[64,64]{0,1:T(8,128)S(1)} %fusion.28), channel_id=1, replica_groups=mesh['tm'=32,'lon'=16] {'tm'}, use_global_device_ids=true, to_apply=%region_2.3 | all-reduce | flops 4096 | bytes 32768 | tf_op jit(solution)/shard_map/psum | solution.py:63
  344.2 5.8 cholesky.16
  350.0 0.6 compare_reduce_fusion
  350.7 0.7 fusion.18
  351.3 4.9 custom-call.7
  356.2 0.9 broadcast_multiply_fusion
  357.1 2.3 fusion.23
  359.4 268.1 %all-reduce.2 = bf16[9216,64]{0,1:T(8,128)(2,1)S(1)} all-reduce(f32[9216,64]{0,1:T(8,128)} %fusion.23), channel_id=1, replica_groups=mesh['tm'=32,'lon'=16] {'tm'}, use_global_device_ids=true, to_apply=%region_5.6 | all-reduce | flops 589824 | bytes 3538944 | tf_op jit(solution)/shard_map/psum | solution.py:69
  627.6 0.8 convolution_convert_fusion
  628.4 2.4 copy.23
  630.8 4.3 copy.24
  (7 shorter events, 0.2 us)
Async XLA Ops:
  0.6 21.6 %copy-start = (bf16[128,18,512]{2,0,1:T(8,128)(2,1)S(1)}, bf16[128,18,512]{2,0,1:T(8,128)(2,1)}, u32[]{:S(2)}) copy-start(bf16[128,18,512]{2,0,1:T(8,128)(2,1)} %param.2) | copy-start | bytes 7077892
  1.9 10.1 %collective-permute-start = (bf16[15,18,512]{2,0,1:T(8,128)(2,1)S(1)}, bf16[15,18,512]{2,0,1:T(8,128)(2,1)S(1)}, u32[]{:S(2)}, u32[]{:S(2)}) collective-permute-start(bf16[15,18,512]{2,0,1:T(8,128)(2,1)S(1)} %get-tuple-element.12), channel_id=1, source_target_pairs={{0,16},{16,32},{32,48},{48,64},{64,80},{80,96},{96,112},{112,128},... | collective-permute-start | bytes 829448 | tf_op jit(solution)/shard_map/ppermute | solution.py:20
  5.8 16.5 %collective-permute-start.1 = (bf16[15,18,512]{2,0,1:T(8,128)(2,1)S(1)}, bf16[15,18,512]{2,0,1:T(8,128)(2,1)S(1)}, u32[]{:S(2)}, u32[]{:S(2)}) collective-permute-start(bf16[15,18,512]{2,0,1:T(8,128)(2,1)S(1)} %get-tuple-element.13), channel_id=1, source_target_pairs={{16,0},{32,16},{48,32},{64,48},{80,64},{96,80},{112,96},{128,112},... | collective-permute-start | bytes 829448 | tf_op jit(solution)/shard_map/ppermute | solution.py:23
  22.4 16.4 %collective-permute-start.2 = (bf16[158,1,512]{2,0,1:T(8,128)(2,1)S(1)}, bf16[158,1,512]{2,0,1:T(8,128)(2,1)S(1)}, u32[]{:S(2)}, u32[]{:S(2)}) collective-permute-start(bf16[158,1,512]{2,0,1:T(8,128)(2,1)S(1)} %get-tuple-element.10), channel_id=1, source_target_pairs={{0,1},{1,2},{2,3},{3,4},{4,5},{5,6},{6,7},{7,8},{8,9},{9,10},{10,1... | collective-permute-start | bytes 485384 | tf_op jit(solution)/shard_map/ppermute | solution.py:20
  24.3 20.6 %collective-permute-start.3 = (bf16[158,1,512]{2,0,1:T(8,128)(2,1)S(1)}, bf16[158,1,512]{2,0,1:T(8,128)(2,1)S(1)}, u32[]{:S(2)}, u32[]{:S(2)}) collective-permute-start(bf16[158,1,512]{2,0,1:T(8,128)(2,1)S(1)} %get-tuple-element.11), channel_id=1, source_target_pairs={{1,0},{2,1},{3,2},{4,3},{5,4},{6,5},{7,6},{8,7},{9,8},{10,9},{11,1... | collective-permute-start | bytes 485384 | tf_op jit(solution)/shard_map/ppermute | solution.py:23
